TPU v7x, 128 devices: a whole 4x4x4 slice. The times are simulated.
128 devices in a mesh: cluster: 8 (over z, core), seq: 16 (over x, y).
Axes of the slice: x: 4, y: 4, z: 4, core: 2. Of those that a mesh axis runs over, the one named last changes fastest.
Arguments:
- nodes: bfloat16 [65536, 1024], P(('cluster', 'seq')), may hold values from -48 to 48
- w_qkv: bfloat16 [1024, 3072], replicated, may hold values from -0.1875 to 0.1875
- w_out: bfloat16 [1024, 1024], replicated, may hold values from -1.5 to 1.5
- kv_ids: int32 [512, 16], P('cluster'), may hold values from 0 to 511, as said below
- counts: int32 [512], P('cluster'), may hold values from 13 to 16, as said below
Outputs:
- attended_out: bfloat16 [65536, 1024], P(('cluster', 'seq'))
Inputs may be any that keep to these rules, and one draw needn't show every extreme that they name: `kv_ids`: entries name blocks; the cluster of block b is b // 64. For query block q, entry 0 is q itself, entries 0 to 11 are distinct blocks of q's cluster, and the last 4 entries are distinct blocks of other clusters. Over all entries of the query blocks of one cluster, at most 16 distinct blocks of any one other cluster are named, and exactly 16 for some pair of clusters. The first counts[q] entries of query block q's list are valid, the others are padding.
All inputs are finite; a program needn't handle non-finite values.
Results may differ from a plain program's by a relative error of at most 0.012.
Values may be sent and summed in bfloat16 or wider, within the bound.
A program may use at most 128 MiB of HBM per device.

v0:
```python
import jax
import jax.numpy as jnp
from jax import lax
from jax.sharding import PartitionSpec as P

D = 1024
HEADS = 16
HD = 64
BLK = 128
KVB = 16
REMOTE = 4


def on_device(nodes, w_qkv, w_out, kv_ids, counts):
    seq_size = lax.axis_size("seq")
    node_rows = nodes.shape[0]
    heads_dev = HEADS // seq_size
    w_grouped = w_qkv.reshape(D, seq_size, heads_dev, 3, HD)
    w_query = w_grouped[:, :, :, 0].reshape(D, seq_size, heads_dev * HD)
    w_keyval = w_grouped[:, :, :, 1:].reshape(D, seq_size, heads_dev * 2 * HD)
    query_proj = jnp.einsum(
        "rd,dsf->srf", nodes, w_query, preferred_element_type=jnp.float32
    ).astype(jnp.bfloat16)
    keyval_proj = jnp.einsum(
        "rd,dsf->srf", nodes, w_keyval, preferred_element_type=jnp.float32
    ).astype(jnp.bfloat16)
    query_recv, keyval_recv = (
        lax.all_to_all(query_proj, "seq", split_axis=0, concat_axis=0, tiled=True),
        lax.all_to_all(keyval_proj, "seq", split_axis=0, concat_axis=0, tiled=True),
    )
    cluster_rows = seq_size * node_rows
    block_count = cluster_rows // BLK
    queries = query_recv.reshape(block_count, BLK, heads_dev, HD)
    keyval_blocks = keyval_recv.reshape(block_count, BLK, heads_dev, 2, HD)
    key_table = jnp.transpose(keyval_blocks[:, :, :, 0], (0, 2, 3, 1))
    value_table = jnp.transpose(keyval_blocks[:, :, :, 1], (0, 2, 1, 3))
    cluster = lax.axis_index("cluster")
    local_ids = kv_ids[:, : KVB - REMOTE] - cluster * block_count
    remote_ids = kv_ids[:, KVB - REMOTE :]
    slot_ids = jnp.arange(KVB, dtype=jnp.int32)
    is_valid = slot_ids[None, :] < counts[:, None]
    far_keys, far_values = (
        lax.all_gather(key_table, "cluster", axis=0, tiled=True),
        lax.all_gather(value_table, "cluster", axis=0, tiled=True),
    )
    groups = block_count // 4
    scale = HD ** (-0.5)

    def attend(packed):
        query_blk, near_ids, far_ids, valid_blk = packed
        near_k = key_table[near_ids]
        far_k = far_keys[far_ids]
        near_v = value_table[near_ids]
        far_v = far_values[far_ids]
        near_scores = (
            jnp.einsum("qahe,qjhek->qhajk", query_blk, near_k, preferred_element_type=jnp.float32)
            * scale
        )
        far_scores = (
            jnp.einsum("qahe,qjhek->qhajk", query_blk, far_k, preferred_element_type=jnp.float32)
            * scale
        )
        near_scores = jnp.where(valid_blk[:, None, None, : KVB - REMOTE, None], near_scores, -1e30)
        far_scores = jnp.where(valid_blk[:, None, None, KVB - REMOTE :, None], far_scores, -1e30)
        row_top = jnp.maximum(
            jnp.max(near_scores, axis=(3, 4), keepdims=True),
            jnp.max(far_scores, axis=(3, 4), keepdims=True),
        )
        near_exp = jnp.exp(near_scores - row_top)
        far_exp = jnp.exp(far_scores - row_top)
        row_total = jnp.sum(near_exp, axis=(3, 4), keepdims=True) + jnp.sum(
            far_exp, axis=(3, 4), keepdims=True
        )
        near_weight = (near_exp / row_total).astype(jnp.bfloat16)
        far_weight = (far_exp / row_total).astype(jnp.bfloat16)
        summed = jnp.einsum(
            "qhajk,qjhke->qahe", near_weight, near_v, preferred_element_type=jnp.float32
        )
        summed = summed + jnp.einsum(
            "qhajk,qjhke->qahe", far_weight, far_v, preferred_element_type=jnp.float32
        )
        return summed.astype(jnp.bfloat16)

    attended = lax.map(
        attend,
        (
            queries.reshape(groups, 4, BLK, heads_dev, HD),
            local_ids.reshape(groups, 4, KVB - REMOTE),
            remote_ids.reshape(groups, 4, REMOTE),
            is_valid.reshape(groups, 4, KVB),
        ),
    )
    attended = attended.reshape(seq_size, node_rows, heads_dev * HD)
    returned = lax.all_to_all(attended, "seq", split_axis=0, concat_axis=0, tiled=True)
    w_split = w_out.reshape(seq_size, heads_dev * HD, D)
    return jnp.einsum("srf,sfd->rd", returned, w_split, preferred_element_type=jnp.float32).astype(
        jnp.bfloat16
    )


def solution(mesh):
    placed = (P(("cluster", "seq"), None), P(), P(), P("cluster", None), P("cluster"))
    return jax.shard_map(
        on_device,
        mesh=mesh,
        in_specs=placed,
        out_specs=P(("cluster", "seq"), None),
        check_vma=False,
    )
```

profile of v0, /device:TPU:0, one launch (start us, length us, event | category | flops | bytes accessed | tf_op | source)
XLA Modules:
  0.0 600.5 jit_solution(15980403184799001119)
XLA Ops:
  6.5 8.8 %copy.22 = bf16[1024,3072]{0,1:T(8,128)(2,1)} copy(bf16[1024,3072]{1,0:T(8,128)(2,1)} %param.8) | data formatting | bytes 12582912 | tf_op args[1]
  20.5 35.2 %all_to_all.15 = bf16[16,512,128]{1,2,0:T(8,128)(2,1)S(1)} all-to-all(bf16[16,512,128]{1,2,0:T(8,128)(2,1)S(1)} %convert_bitcast_fusion), channel_id=1, replica_groups=mesh['cluster'=8,'seq'=16] {'seq'}, dimensions={0} | all-to-all | bytes 4194304 | tf_op jit(solution)/shard_map/all_to_all | solution.py:29
  76.2 14.9 %all-to-all-done.1 = bf16[16,512,64]{1,2,0:T(8,128)(2,1)S(1)} async-done(((bf16[16,512,64]{1,2,0:T(8,128)(2,1)}), bf16[16,512,64]{1,2,0:T(8,128)(2,1)S(1)}, u32[]{:S(2)}, u32[]{:S(2)}) %all-to-all-start.1) | async-done | bytes 1048608 | tf_op jit(solution)/shard_map/all_to_all | solution.py:28
  97.6 18.4 %all-gather.6.cloned.1.call-done = bf16[512,128,1,1,64]{1,0,4,3,2:T(8,128)(2,1)} async-done(((bf16[64,128,1,1,64]{1,0,4,3,2:T(8,128)(2,1)}), bf16[512,128,1,1,64]{1,0,4,3,2:T(8,128)(2,1)}) %all-gather.6.cloned.1.call-update) | async-done | bytes 8388624 | tf_op jit(solution)/shard_map/all_gather | solution.py:44
  115.9 17.9 %copy.30 = bf16[512,1,128,64]{3,2,1,0:T(8,128)(2,1)} copy(bf16[512,1,128,64]{2,0,3,1:T(8,128)(2,1)} %bitcast.149) | data formatting | bytes 16777216 | tf_op jit(solution)/shard_map/while | solution.py:84
  133.9 33.7 %all-gather.4.cloned.1.call-done = bf16[512,1,64,128]{3,0,2,1:T(8,128)(2,1)} async-done(((bf16[64,1,64,128]{3,0,2,1:T(8,128)(2,1)}), bf16[512,1,64,128]{3,0,2,1:T(8,128)(2,1)}) %all-gather.4.cloned.1.call-update) | async-done | bytes 8388624 | tf_op jit(solution)/shard_map/all_gather | solution.py:43
  167.6 12.0 %copy.29 = bf16[512,1,64,128]{3,2,1,0:T(8,128)(2,1)} copy(bf16[512,1,64,128]{3,0,2,1:T(8,128)(2,1)} %all-gather.4.cloned.1.call-done) | data formatting | bytes 16777216 | tf_op jit(solution)/shard_map/while | solution.py:84
  179.6 386.2 %while.10 = (s32[]{:T(128)}, bf16[16,4,128,1,64]{2,1,4,0,3:T(4,128)(2,1)}, s32[16,4,12]{2,1,0:T(4,128)S(1)}, bf16[64,1,128,64]{3,2,1,0:T(8,128)(2,1)}, pred[16,4...) while((s32[]{:T(128)}, ...), condition=%wide.region_5.6_spmd, body=%wide.region_0.5_spmd.sunk | while | flops 280036544 | bytes 32221496 | solution.py:84
  185.4 7.2 %gather_fusion = bf16[16,128,64]{2,1,0:T(8,128)(2,1)} fusion(bf16[512,128,64]{2,1,0:T(8,128)(2,1)} %bitcast.144, s32[1024]{0:T(1024)S(1)} %pad_clamp_fusion.4), kind=kCustom, calls=%fused_computation.3.clone.1 | custom fusion | bytes 524352 | tf_op jit(solution)/shard_map/while/body/eval_jaxpr/gather | solution.py:54
  209.6 7.2 %gather_fusion = bf16[16,128,64]{2,1,0:T(8,128)(2,1)} fusion(bf16[512,128,64]{2,1,0:T(8,128)(2,1)} %bitcast.144, s32[1024]{0:T(1024)S(1)} %pad_clamp_fusion.4), kind=kCustom, calls=%fused_computation.3.clone.1 | custom fusion | bytes 524352 | tf_op jit(solution)/shard_map/while/body/eval_jaxpr/gather | solution.py:54
  233.7 7.2 %gather_fusion = bf16[16,128,64]{2,1,0:T(8,128)(2,1)} fusion(bf16[512,128,64]{2,1,0:T(8,128)(2,1)} %bitcast.144, s32[1024]{0:T(1024)S(1)} %pad_clamp_fusion.4), kind=kCustom, calls=%fused_computation.3.clone.1 | custom fusion | bytes 524352 | tf_op jit(solution)/shard_map/while/body/eval_jaxpr/gather | solution.py:54
  257.9 7.2 %gather_fusion = bf16[16,128,64]{2,1,0:T(8,128)(2,1)} fusion(bf16[512,128,64]{2,1,0:T(8,128)(2,1)} %bitcast.144, s32[1024]{0:T(1024)S(1)} %pad_clamp_fusion.4), kind=kCustom, calls=%fused_computation.3.clone.1 | custom fusion | bytes 524352 | tf_op jit(solution)/shard_map/while/body/eval_jaxpr/gather | solution.py:54
  282.0 7.2 %gather_fusion = bf16[16,128,64]{2,1,0:T(8,128)(2,1)} fusion(bf16[512,128,64]{2,1,0:T(8,128)(2,1)} %bitcast.144, s32[1024]{0:T(1024)S(1)} %pad_clamp_fusion.4), kind=kCustom, calls=%fused_computation.3.clone.1 | custom fusion | bytes 524352 | tf_op jit(solution)/shard_map/while/body/eval_jaxpr/gather | solution.py:54
  306.1 7.2 %gather_fusion = bf16[16,128,64]{2,1,0:T(8,128)(2,1)} fusion(bf16[512,128,64]{2,1,0:T(8,128)(2,1)} %bitcast.144, s32[1024]{0:T(1024)S(1)} %pad_clamp_fusion.4), kind=kCustom, calls=%fused_computation.3.clone.1 | custom fusion | bytes 524352 | tf_op jit(solution)/shard_map/while/body/eval_jaxpr/gather | solution.py:54
  330.2 7.2 %gather_fusion = bf16[16,128,64]{2,1,0:T(8,128)(2,1)} fusion(bf16[512,128,64]{2,1,0:T(8,128)(2,1)} %bitcast.144, s32[1024]{0:T(1024)S(1)} %pad_clamp_fusion.4), kind=kCustom, calls=%fused_computation.3.clone.1 | custom fusion | bytes 524352 | tf_op jit(solution)/shard_map/while/body/eval_jaxpr/gather | solution.py:54
  354.3 7.2 %gather_fusion = bf16[16,128,64]{2,1,0:T(8,128)(2,1)} fusion(bf16[512,128,64]{2,1,0:T(8,128)(2,1)} %bitcast.144, s32[1024]{0:T(1024)S(1)} %pad_clamp_fusion.4), kind=kCustom, calls=%fused_computation.3.clone.1 | custom fusion | bytes 524352 | tf_op jit(solution)/shard_map/while/body/eval_jaxpr/gather | solution.py:54
  378.5 7.2 %gather_fusion = bf16[16,128,64]{2,1,0:T(8,128)(2,1)} fusion(bf16[512,128,64]{2,1,0:T(8,128)(2,1)} %bitcast.144, s32[1024]{0:T(1024)S(1)} %pad_clamp_fusion.4), kind=kCustom, calls=%fused_computation.3.clone.1 | custom fusion | bytes 524352 | tf_op jit(solution)/shard_map/while/body/eval_jaxpr/gather | solution.py:54
  402.7 7.2 %gather_fusion = bf16[16,128,64]{2,1,0:T(8,128)(2,1)} fusion(bf16[512,128,64]{2,1,0:T(8,128)(2,1)} %bitcast.144, s32[1024]{0:T(1024)S(1)} %pad_clamp_fusion.4), kind=kCustom, calls=%fused_computation.3.clone.1 | custom fusion | bytes 524352 | tf_op jit(solution)/shard_map/while/body/eval_jaxpr/gather | solution.py:54
  426.8 7.2 %gather_fusion = bf16[16,128,64]{2,1,0:T(8,128)(2,1)} fusion(bf16[512,128,64]{2,1,0:T(8,128)(2,1)} %bitcast.144, s32[1024]{0:T(1024)S(1)} %pad_clamp_fusion.4), kind=kCustom, calls=%fused_computation.3.clone.1 | custom fusion | bytes 524352 | tf_op jit(solution)/shard_map/while/body/eval_jaxpr/gather | solution.py:54
  451.0 7.2 %gather_fusion = bf16[16,128,64]{2,1,0:T(8,128)(2,1)} fusion(bf16[512,128,64]{2,1,0:T(8,128)(2,1)} %bitcast.144, s32[1024]{0:T(1024)S(1)} %pad_clamp_fusion.4), kind=kCustom, calls=%fused_computation.3.clone.1 | custom fusion | bytes 524352 | tf_op jit(solution)/shard_map/while/body/eval_jaxpr/gather | solution.py:54
  475.1 7.2 %gather_fusion = bf16[16,128,64]{2,1,0:T(8,128)(2,1)} fusion(bf16[512,128,64]{2,1,0:T(8,128)(2,1)} %bitcast.144, s32[1024]{0:T(1024)S(1)} %pad_clamp_fusion.4), kind=kCustom, calls=%fused_computation.3.clone.1 | custom fusion | bytes 524352 | tf_op jit(solution)/shard_map/while/body/eval_jaxpr/gather | solution.py:54
  499.2 7.2 %gather_fusion = bf16[16,128,64]{2,1,0:T(8,128)(2,1)} fusion(bf16[512,128,64]{2,1,0:T(8,128)(2,1)} %bitcast.144, s32[1024]{0:T(1024)S(1)} %pad_clamp_fusion.4), kind=kCustom, calls=%fused_computation.3.clone.1 | custom fusion | bytes 524352 | tf_op jit(solution)/shard_map/while/body/eval_jaxpr/gather | solution.py:54
  523.4 7.2 %gather_fusion = bf16[16,128,64]{2,1,0:T(8,128)(2,1)} fusion(bf16[512,128,64]{2,1,0:T(8,128)(2,1)} %bitcast.144, s32[1024]{0:T(1024)S(1)} %pad_clamp_fusion.4), kind=kCustom, calls=%fused_computation.3.clone.1 | custom fusion | bytes 524352 | tf_op jit(solution)/shard_map/while/body/eval_jaxpr/gather | solution.py:54
  567.3 24.1 %all_to_all.16 = bf16[16,512,64]{1,2,0:T(8,128)(2,1)S(1)} all-to-all(bf16[16,512,64]{1,2,0:T(8,128)(2,1)S(1)} %reshape.170), channel_id=1, replica_groups=mesh['cluster'=8,'seq'=16] {'seq'}, dimensions={0} | all-to-all | bytes 2097152 | tf_op jit(solution)/shard_map/all_to_all | solution.py:94
  (496 shorter events, 313.4 us)
Async XLA Ops:
  6.5 584.9 %copy-start = (bf16[1024,1024]{1,0:T(8,128)(2,1)S(1)}, bf16[1024,1024]{1,0:T(8,128)(2,1)}, u32[]{:S(2)}) copy-start(bf16[1024,1024]{1,0:T(8,128)(2,1)} %param.9) | copy-start | bytes 6291460
  6.5 109.4 %all-gather.6.cloned.1.call-start = ((), (), s32[]{:S(2)}) async-start(), calls=%async_computation.4 | async-start | bytes 9437184 | tf_op jit(solution)/shard_map/all_gather | solution.py:44
  66.7 100.9 %all-gather.4.cloned.1.call-start = ((), (), s32[]{:S(2)}) async-start(), calls=%async_computation.3 | async-start | bytes 9437184 | tf_op jit(solution)/shard_map/all_gather | solution.py:43
  67.4 7.8 %copy-start.5 = (s32[64,16]{0,1:T(8,128)S(1)}, s32[64,16]{0,1:T(8,128)}, u32[]{:S(2)}) copy-start(s32[64,16]{0,1:T(8,128)} %param.10) | copy-start | bytes 12292
  67.4 7.8 %copy-start.6 = (s32[64]{0:T(128)S(1)}, s32[64]{0:T(128)}, u32[]{:S(2)}) copy-start(s32[64]{0:T(128)} %param.11) | copy-start | bytes 772
  71.3 19.8 %all-to-all-start.1 = ((bf16[16,512,64]{1,2,0:T(8,128)(2,1)}), bf16[16,512,64]{1,2,0:T(8,128)(2,1)S(1)}, u32[]{:S(2)}, u32[]{:S(2)}) async-start(bf16[16,512,64]{1,2,0:T(8,128)(2,1)} %fusion.14), calls=%async_computation.1 | async-start | bytes 2097152 | tf_op jit(solution)/shard_map/all_to_all | solution.py:28
  179.6 14.5 %copy-start.2 = (bf16[64,1,64,128]{3,2,1,0:T(8,128)(2,1)}, bf16[64,1,64,128]{3,2,1,0:T(8,128)(2,1)S(1)}, u32[]{:S(2)}) copy-start(bf16[64,1,64,128]{3,2,1,0:T(8,128)(2,1)S(1)} %get-tuple-element.202) | copy-start | bytes 3145732 | tf_op jit(solution)/shard_map/while
  203.8 14.5 %copy-start.2 = (bf16[64,1,64,128]{3,2,1,0:T(8,128)(2,1)}, bf16[64,1,64,128]{3,2,1,0:T(8,128)(2,1)S(1)}, u32[]{:S(2)}) copy-start(bf16[64,1,64,128]{3,2,1,0:T(8,128)(2,1)S(1)} %get-tuple-element.202) | copy-start | bytes 3145732 | tf_op jit(solution)/shard_map/while
  227.9 14.5 %copy-start.2 = (bf16[64,1,64,128]{3,2,1,0:T(8,128)(2,1)}, bf16[64,1,64,128]{3,2,1,0:T(8,128)(2,1)S(1)}, u32[]{:S(2)}) copy-start(bf16[64,1,64,128]{3,2,1,0:T(8,128)(2,1)S(1)} %get-tuple-element.202) | copy-start | bytes 3145732 | tf_op jit(solution)/shard_map/while
  252.1 14.6 %copy-start.2 = (bf16[64,1,64,128]{3,2,1,0:T(8,128)(2,1)}, bf16[64,1,64,128]{3,2,1,0:T(8,128)(2,1)S(1)}, u32[]{:S(2)}) copy-start(bf16[64,1,64,128]{3,2,1,0:T(8,128)(2,1)S(1)} %get-tuple-element.202) | copy-start | bytes 3145732 | tf_op jit(solution)/shard_map/while
  276.2 14.5 %copy-start.2 = (bf16[64,1,64,128]{3,2,1,0:T(8,128)(2,1)}, bf16[64,1,64,128]{3,2,1,0:T(8,128)(2,1)S(1)}, u32[]{:S(2)}) copy-start(bf16[64,1,64,128]{3,2,1,0:T(8,128)(2,1)S(1)} %get-tuple-element.202) | copy-start | bytes 3145732 | tf_op jit(solution)/shard_map/while
  300.4 14.5 %copy-start.2 = (bf16[64,1,64,128]{3,2,1,0:T(8,128)(2,1)}, bf16[64,1,64,128]{3,2,1,0:T(8,128)(2,1)S(1)}, u32[]{:S(2)}) copy-start(bf16[64,1,64,128]{3,2,1,0:T(8,128)(2,1)S(1)} %get-tuple-element.202) | copy-start | bytes 3145732 | tf_op jit(solution)/shard_map/while
  324.5 14.5 %copy-start.2 = (bf16[64,1,64,128]{3,2,1,0:T(8,128)(2,1)}, bf16[64,1,64,128]{3,2,1,0:T(8,128)(2,1)S(1)}, u32[]{:S(2)}) copy-start(bf16[64,1,64,128]{3,2,1,0:T(8,128)(2,1)S(1)} %get-tuple-element.202) | copy-start | bytes 3145732 | tf_op jit(solution)/shard_map/while
  348.6 14.5 %copy-start.2 = (bf16[64,1,64,128]{3,2,1,0:T(8,128)(2,1)}, bf16[64,1,64,128]{3,2,1,0:T(8,128)(2,1)S(1)}, u32[]{:S(2)}) copy-start(bf16[64,1,64,128]{3,2,1,0:T(8,128)(2,1)S(1)} %get-tuple-element.202) | copy-start | bytes 3145732 | tf_op jit(solution)/shard_map/while
  372.7 14.6 %copy-start.2 = (bf16[64,1,64,128]{3,2,1,0:T(8,128)(2,1)}, bf16[64,1,64,128]{3,2,1,0:T(8,128)(2,1)S(1)}, u32[]{:S(2)}) copy-start(bf16[64,1,64,128]{3,2,1,0:T(8,128)(2,1)S(1)} %get-tuple-element.202) | copy-start | bytes 3145732 | tf_op jit(solution)/shard_map/while
  396.8 14.6 %copy-start.2 = (bf16[64,1,64,128]{3,2,1,0:T(8,128)(2,1)}, bf16[64,1,64,128]{3,2,1,0:T(8,128)(2,1)S(1)}, u32[]{:S(2)}) copy-start(bf16[64,1,64,128]{3,2,1,0:T(8,128)(2,1)S(1)} %get-tuple-element.202) | copy-start | bytes 3145732 | tf_op jit(solution)/shard_map/while
  421.0 14.5 %copy-start.2 = (bf16[64,1,64,128]{3,2,1,0:T(8,128)(2,1)}, bf16[64,1,64,128]{3,2,1,0:T(8,128)(2,1)S(1)}, u32[]{:S(2)}) copy-start(bf16[64,1,64,128]{3,2,1,0:T(8,128)(2,1)S(1)} %get-tuple-element.202) | copy-start | bytes 3145732 | tf_op jit(solution)/shard_map/while
  445.2 14.5 %copy-start.2 = (bf16[64,1,64,128]{3,2,1,0:T(8,128)(2,1)}, bf16[64,1,64,128]{3,2,1,0:T(8,128)(2,1)S(1)}, u32[]{:S(2)}) copy-start(bf16[64,1,64,128]{3,2,1,0:T(8,128)(2,1)S(1)} %get-tuple-element.202) | copy-start | bytes 3145732 | tf_op jit(solution)/shard_map/while
  463.7 3.2 copy-start.4
  469.3 14.5 %copy-start.2 = (bf16[64,1,64,128]{3,2,1,0:T(8,128)(2,1)}, bf16[64,1,64,128]{3,2,1,0:T(8,128)(2,1)S(1)}, u32[]{:S(2)}) copy-start(bf16[64,1,64,128]{3,2,1,0:T(8,128)(2,1)S(1)} %get-tuple-element.202) | copy-start | bytes 3145732 | tf_op jit(solution)/shard_map/while
  493.4 14.5 %copy-start.2 = (bf16[64,1,64,128]{3,2,1,0:T(8,128)(2,1)}, bf16[64,1,64,128]{3,2,1,0:T(8,128)(2,1)S(1)}, u32[]{:S(2)}) copy-start(bf16[64,1,64,128]{3,2,1,0:T(8,128)(2,1)S(1)} %get-tuple-element.202) | copy-start | bytes 3145732 | tf_op jit(solution)/shard_map/while
  517.6 14.5 %copy-start.2 = (bf16[64,1,64,128]{3,2,1,0:T(8,128)(2,1)}, bf16[64,1,64,128]{3,2,1,0:T(8,128)(2,1)S(1)}, u32[]{:S(2)}) copy-start(bf16[64,1,64,128]{3,2,1,0:T(8,128)(2,1)S(1)} %get-tuple-element.202) | copy-start | bytes 3145732 | tf_op jit(solution)/shard_map/while
  536.1 3.2 copy-start.4
  541.7 14.5 %copy-start.2 = (bf16[64,1,64,128]{3,2,1,0:T(8,128)(2,1)}, bf16[64,1,64,128]{3,2,1,0:T(8,128)(2,1)S(1)}, u32[]{:S(2)}) copy-start(bf16[64,1,64,128]{3,2,1,0:T(8,128)(2,1)S(1)} %get-tuple-element.202) | copy-start | bytes 3145732 | tf_op jit(solution)/shard_map/while
  (47 other events, 99.8 us)
Sparse Core Ops, SparseCore 0:
  66.8 49.0 all-gather.5
  117.6 49.9 all-gather.3
where the time goes:
time: 605 us; the launch traced here: 601 us
  local copies, waits for them, and re-layouts  364 us (60%)
  matrix products  74.1 us (12%)
  waiting for transfers between devices  67.7 us (11%)
  blocking collectives  59.3 us (10%)
  other arithmetic  16.9 us (3%)
  between operations  13.5 us (2%)
    gather x16, local copies, waits for them, and re-layouts, attend(): far_v = far_values[far_ids]  115 us
    gather x16, local copies, waits for them, and re-layouts, attend(): far_k = far_keys[far_ids]  63.7 us
    gather x16, local copies, waits for them, and re-layouts, attend(): near_v = value_table[near_ids]  57.6 us
    while x4, local copies, waits for them, and re-layouts, on_device(): lax.map(attend, (queries.reshape(groups, 4, BLK, heads_dev, HD), local_id...  35.3 us
    all_to_all x1, blocking collectives, on_device(): lax.all_to_all(keyval_proj, 'seq', split_axis=0, concat_axis=0, tiled=True)  35.2 us
    dot_general x16, matrix products, attend(): jnp.einsum('qahe,qjhek->qhajk', query_blk, near_k, preferred_element_type...  34.2 us
    all_gather x1, waiting for transfers between devices, on_device(): lax.all_gather(key_table, 'cluster', axis=0, tiled=True)  33.7 us
    gather x16, local copies, waits for them, and re-layouts, attend(): near_k = key_table[near_ids]  24.9 us
  transfers between devices with their start and end apart: 3, of which 3 were waited for; matrix products, arithmetic and copies ran while one was open for 5% of the time, Pallas kernels for 0%

commit v1 on v0

--- a/solution.py
+++ b/solution.py
@@ -2,6 +2,7 @@
 import jax.numpy as jnp
 from jax import lax
 from jax.sharding import PartitionSpec as P
+from jax.lax import all_to_all, axis_size
 
 D = 1024
 HEADS = 16
@@ -12,6 +13,12 @@
 
 
 def on_device(nodes, w_qkv, w_out, kv_ids, counts):
+
+    def divide_boxes_on_mesh(lane_axis, inner_x):
+        b_next = jnp.stack([inner_x for _ in range(axis_size(lane_axis))], 0)
+        passed = all_to_all(b_next, axis_name=lane_axis, split_axis=0, concat_axis=0)
+        return jnp.concatenate(passed, 0)
+
     seq_size = lax.axis_size("seq")
     node_rows = nodes.shape[0]
     heads_dev = HEADS // seq_size
@@ -40,7 +47,7 @@
     slot_ids = jnp.arange(KVB, dtype=jnp.int32)
     is_valid = slot_ids[None, :] < counts[:, None]
     far_keys, far_values = (
-        lax.all_gather(key_table, "cluster", axis=0, tiled=True),
+        divide_boxes_on_mesh("cluster", key_table),
         lax.all_gather(value_table, "cluster", axis=0, tiled=True),
     )
     groups = block_count // 4

time: 605 us -> 629 us (1.040)
  waiting for transfers between devices: 67.7 us -> 90.5 us
    all_to_all x0 -> x1, waiting for transfers between devices: none -> 54.1 us  [divide_boxes_on_mesh(): all_to_all(b_next, axis_name=lane_axis, split_axis=0, concat_axis=0)]
    all_gather x1 -> x0, waiting for transfers between devices: 33.7 us -> none  [on_device(): lax.all_gather(key_table, 'cluster', axis=0, tiled=True)]
    while x4 -> x3, local copies, waits for them, and re-layouts: 35.3 us -> 22.9 us  [on_device(): lax.map(attend, (queries.reshape(groups, 4, BLK, heads_dev, HD), local_id...]
  transfers between devices with their start and end apart: 3 -> 3, of which waited for: 3 -> 3; matrix products, arithmetic and copies ran while one was open for 5% -> 6% of each run, Pallas kernels for 0% -> 0%
where the time goes in v1:
time: 629 us; the launch traced here: 625 us
  local copies, waits for them, and re-layouts  360 us (57%)
  waiting for transfers between devices  90.5 us (14%)
  matrix products  74.1 us (12%)
  blocking collectives  58.7 us (9%)
  other arithmetic  16.9 us (3%)
  between operations  13.5 us (2%)
  starting transfers between devices  9.78 us (2%)
    gather x16, local copies, waits for them, and re-layouts, attend(): far_v = far_values[far_ids]  115 us
    gather x16, local copies, waits for them, and re-layouts, attend(): far_k = far_keys[far_ids]  63.7 us
    gather x16, local copies, waits for them, and re-layouts, attend(): near_v = value_table[near_ids]  57.7 us
    all_to_all x1, waiting for transfers between devices, divide_boxes_on_mesh(): all_to_all(b_next, axis_name=lane_axis, split_axis=0, concat_axis=0)  54.1 us
    all_to_all x1, blocking collectives, on_device(): lax.all_to_all(keyval_proj, 'seq', split_axis=0, concat_axis=0, tiled=True)  35.2 us
    dot_general x16, matrix products, attend(): jnp.einsum('qahe,qjhek->qhajk', query_blk, near_k, preferred_element_type...  34.2 us
    gather x16, local copies, waits for them, and re-layouts, attend(): near_k = key_table[near_ids]  24.9 us
    all_to_all x1, blocking collectives, on_device(): lax.all_to_all(attended, 'seq', split_axis=0, concat_axis=0, tiled=True)  23.5 us
  transfers between devices with their start and end apart: 3, of which 3 were waited for; matrix products, arithmetic and copies ran while one was open for 6% of the time, Pallas kernels for 0%

profile of v1, /device:TPU:0, one launch (start us, length us, event | category | flops | bytes accessed | tf_op | source)
XLA Modules:
  0.0 624.6 jit_solution(9404751591347741222)
XLA Ops:
  6.5 8.8 %copy.37 = bf16[1024,3072]{0,1:T(8,128)(2,1)} copy(bf16[1024,3072]{1,0:T(8,128)(2,1)} %param.8) | data formatting | bytes 12582912 | tf_op args[1]
  20.5 35.2 %all_to_all.20 = bf16[16,512,128]{1,2,0:T(8,128)(2,1)S(1)} all-to-all(bf16[16,512,128]{1,2,0:T(8,128)(2,1)S(1)} %convert_bitcast_fusion), channel_id=1, replica_groups=mesh['cluster'=8,'seq'=16] {'seq'}, dimensions={0} | all-to-all | bytes 4194304 | tf_op jit(solution)/shard_map/all_to_all | solution.py:36
  77.2 13.6 %all-to-all-done.1 = bf16[16,512,64]{1,2,0:T(8,128)(2,1)} async-done(((bf16[16,512,64]{1,2,0:T(8,128)(2,1)}), bf16[16,512,64]{1,2,0:T(8,128)(2,1)}, u32[]{:S(2)}, u32[]{:S(2)}) %all-to-all-start.1) | async-done | bytes 1048608 | tf_op jit(solution)/shard_map/all_to_all | solution.py:35
  110.1 22.9 %all-gather.3.cloned.1.call-done = bf16[512,128,1,1,64]{1,0,4,3,2:T(8,128)(2,1)} async-done(((bf16[64,128,1,1,64]{1,0,4,3,2:T(8,128)(2,1)}), bf16[512,128,1,1,64]{1,0,4,3,2:T(8,128)(2,1)}) %all-gather.3.cloned.1.call-update) | async-done | bytes 8388624 | tf_op jit(solution)/shard_map/all_gather | solution.py:51
  133.0 17.6 %copy.46 = bf16[512,1,128,64]{3,2,1,0:T(8,128)(2,1)} copy(bf16[512,1,128,64]{2,0,3,1:T(8,128)(2,1)} %bitcast.154) | data formatting | bytes 16777216 | tf_op jit(solution)/shard_map/while | solution.py:91
  150.6 54.1 %all-to-all-done.2 = bf16[8,64,1,64,128]{4,3,1,2,0:T(8,128)(2,1)} async-done(((bf16[8,64,1,64,128]{4,3,1,2,0:T(8,128)(2,1)}), bf16[8,64,1,64,128]{4,3,1,2,0:T(8,128)(2,1)}, u32[]{:S(2)}, u32[]{:S(2)}) %all-to-all-start.2) | async-done | bytes 8388640 | tf_op jit(solution)/shard_map/all_to_all | solution.py:19
  204.7 385.8 %while.10 = (s32[]{:T(128)}, bf16[16,4,128,1,64]{2,1,4,0,3:T(4,128)(2,1)}, s32[16,4,12]{2,1,0:T(4,128)S(1)}, bf16[64,1,128,64]{3,2,1,0:T(8,128)(2,1)}, pred[16,4...) while((s32[]{:T(128)}, ...), condition=%wide.region_5.6_spmd, body=%wide.region_0.5_spmd.sunk | while | flops 280036544 | bytes 32221496 | solution.py:91
  210.4 7.2 %gather_fusion = bf16[16,128,64]{2,1,0:T(8,128)(2,1)} fusion(bf16[512,128,64]{2,1,0:T(8,128)(2,1)} %bitcast.150, s32[1024]{0:T(1024)S(1)} %pad_clamp_fusion.4), kind=kCustom, calls=%fused_computation.3.clone.1 | custom fusion | bytes 524352 | tf_op jit(solution)/shard_map/while/body/eval_jaxpr/gather | solution.py:61
  234.6 7.2 %gather_fusion = bf16[16,128,64]{2,1,0:T(8,128)(2,1)} fusion(bf16[512,128,64]{2,1,0:T(8,128)(2,1)} %bitcast.150, s32[1024]{0:T(1024)S(1)} %pad_clamp_fusion.4), kind=kCustom, calls=%fused_computation.3.clone.1 | custom fusion | bytes 524352 | tf_op jit(solution)/shard_map/while/body/eval_jaxpr/gather | solution.py:61
  258.6 7.2 %gather_fusion = bf16[16,128,64]{2,1,0:T(8,128)(2,1)} fusion(bf16[512,128,64]{2,1,0:T(8,128)(2,1)} %bitcast.150, s32[1024]{0:T(1024)S(1)} %pad_clamp_fusion.4), kind=kCustom, calls=%fused_computation.3.clone.1 | custom fusion | bytes 524352 | tf_op jit(solution)/shard_map/while/body/eval_jaxpr/gather | solution.py:61
  282.8 7.2 %gather_fusion = bf16[16,128,64]{2,1,0:T(8,128)(2,1)} fusion(bf16[512,128,64]{2,1,0:T(8,128)(2,1)} %bitcast.150, s32[1024]{0:T(1024)S(1)} %pad_clamp_fusion.4), kind=kCustom, calls=%fused_computation.3.clone.1 | custom fusion | bytes 524352 | tf_op jit(solution)/shard_map/while/body/eval_jaxpr/gather | solution.py:61
  306.8 7.2 %gather_fusion = bf16[16,128,64]{2,1,0:T(8,128)(2,1)} fusion(bf16[512,128,64]{2,1,0:T(8,128)(2,1)} %bitcast.150, s32[1024]{0:T(1024)S(1)} %pad_clamp_fusion.4), kind=kCustom, calls=%fused_computation.3.clone.1 | custom fusion | bytes 524352 | tf_op jit(solution)/shard_map/while/body/eval_jaxpr/gather | solution.py:61
  331.0 7.2 %gather_fusion = bf16[16,128,64]{2,1,0:T(8,128)(2,1)} fusion(bf16[512,128,64]{2,1,0:T(8,128)(2,1)} %bitcast.150, s32[1024]{0:T(1024)S(1)} %pad_clamp_fusion.4), kind=kCustom, calls=%fused_computation.3.clone.1 | custom fusion | bytes 524352 | tf_op jit(solution)/shard_map/while/body/eval_jaxpr/gather | solution.py:61
  355.1 7.2 %gather_fusion = bf16[16,128,64]{2,1,0:T(8,128)(2,1)} fusion(bf16[512,128,64]{2,1,0:T(8,128)(2,1)} %bitcast.150, s32[1024]{0:T(1024)S(1)} %pad_clamp_fusion.4), kind=kCustom, calls=%fused_computation.3.clone.1 | custom fusion | bytes 524352 | tf_op jit(solution)/shard_map/while/body/eval_jaxpr/gather | solution.py:61
  379.2 7.2 %gather_fusion = bf16[16,128,64]{2,1,0:T(8,128)(2,1)} fusion(bf16[512,128,64]{2,1,0:T(8,128)(2,1)} %bitcast.150, s32[1024]{0:T(1024)S(1)} %pad_clamp_fusion.4), kind=kCustom, calls=%fused_computation.3.clone.1 | custom fusion | bytes 524352 | tf_op jit(solution)/shard_map/while/body/eval_jaxpr/gather | solution.py:61
  403.3 7.2 %gather_fusion = bf16[16,128,64]{2,1,0:T(8,128)(2,1)} fusion(bf16[512,128,64]{2,1,0:T(8,128)(2,1)} %bitcast.150, s32[1024]{0:T(1024)S(1)} %pad_clamp_fusion.4), kind=kCustom, calls=%fused_computation.3.clone.1 | custom fusion | bytes 524352 | tf_op jit(solution)/shard_map/while/body/eval_jaxpr/gather | solution.py:61
  427.5 7.2 %gather_fusion = bf16[16,128,64]{2,1,0:T(8,128)(2,1)} fusion(bf16[512,128,64]{2,1,0:T(8,128)(2,1)} %bitcast.150, s32[1024]{0:T(1024)S(1)} %pad_clamp_fusion.4), kind=kCustom, calls=%fused_computation.3.clone.1 | custom fusion | bytes 524352 | tf_op jit(solution)/shard_map/while/body/eval_jaxpr/gather | solution.py:61
  451.6 7.2 %gather_fusion = bf16[16,128,64]{2,1,0:T(8,128)(2,1)} fusion(bf16[512,128,64]{2,1,0:T(8,128)(2,1)} %bitcast.150, s32[1024]{0:T(1024)S(1)} %pad_clamp_fusion.4), kind=kCustom, calls=%fused_computation.3.clone.1 | custom fusion | bytes 524352 | tf_op jit(solution)/shard_map/while/body/eval_jaxpr/gather | solution.py:61
  475.7 7.2 %gather_fusion = bf16[16,128,64]{2,1,0:T(8,128)(2,1)} fusion(bf16[512,128,64]{2,1,0:T(8,128)(2,1)} %bitcast.150, s32[1024]{0:T(1024)S(1)} %pad_clamp_fusion.4), kind=kCustom, calls=%fused_computation.3.clone.1 | custom fusion | bytes 524352 | tf_op jit(solution)/shard_map/while/body/eval_jaxpr/gather | solution.py:61
  499.8 7.2 %gather_fusion = bf16[16,128,64]{2,1,0:T(8,128)(2,1)} fusion(bf16[512,128,64]{2,1,0:T(8,128)(2,1)} %bitcast.150, s32[1024]{0:T(1024)S(1)} %pad_clamp_fusion.4), kind=kCustom, calls=%fused_computation.3.clone.1 | custom fusion | bytes 524352 | tf_op jit(solution)/shard_map/while/body/eval_jaxpr/gather | solution.py:61
  523.9 7.2 %gather_fusion = bf16[16,128,64]{2,1,0:T(8,128)(2,1)} fusion(bf16[512,128,64]{2,1,0:T(8,128)(2,1)} %bitcast.150, s32[1024]{0:T(1024)S(1)} %pad_clamp_fusion.4), kind=kCustom, calls=%fused_computation.3.clone.1 | custom fusion | bytes 524352 | tf_op jit(solution)/shard_map/while/body/eval_jaxpr/gather | solution.py:61
  548.0 7.2 %gather_fusion = bf16[16,128,64]{2,1,0:T(8,128)(2,1)} fusion(bf16[512,128,64]{2,1,0:T(8,128)(2,1)} %bitcast.150, s32[1024]{0:T(1024)S(1)} %pad_clamp_fusion.4), kind=kCustom, calls=%fused_computation.3.clone.1 | custom fusion | bytes 524352 | tf_op jit(solution)/shard_map/while/body/eval_jaxpr/gather | solution.py:61
  572.1 7.2 %gather_fusion = bf16[16,128,64]{2,1,0:T(8,128)(2,1)} fusion(bf16[512,128,64]{2,1,0:T(8,128)(2,1)} %bitcast.150, s32[1024]{0:T(1024)S(1)} %pad_clamp_fusion.4), kind=kCustom, calls=%fused_computation.3.clone.1 | custom fusion | bytes 524352 | tf_op jit(solution)/shard_map/while/body/eval_jaxpr/gather | solution.py:61
  591.9 23.5 %all_to_all.21 = bf16[16,512,64]{1,2,0:T(8,128)(2,1)S(1)} all-to-all(bf16[16,512,64]{1,2,0:T(8,128)(2,1)S(1)} %reshape.177), channel_id=1, replica_groups=mesh['cluster'=8,'seq'=16] {'seq'}, dimensions={0} | all-to-all | bytes 2097152 | tf_op jit(solution)/shard_map/all_to_all | solution.py:101
  (496 shorter events, 320.0 us)
Async XLA Ops:
  6.5 608.9 %copy-start = (bf16[1024,1024]{1,0:T(8,128)(2,1)S(1)}, bf16[1024,1024]{1,0:T(8,128)(2,1)}, u32[]{:S(2)}) copy-start(bf16[1024,1024]{1,0:T(8,128)(2,1)} %param.9) | copy-start | bytes 6291460
  6.5 126.4 %all-gather.3.cloned.1.call-start = ((), (), s32[]{:S(2)}) async-start(), calls=%async_computation.4 | async-start | bytes 9437184 | tf_op jit(solution)/shard_map/all_gather | solution.py:51
  70.9 19.9 %all-to-all-start.1 = ((bf16[16,512,64]{1,2,0:T(8,128)(2,1)}), bf16[16,512,64]{1,2,0:T(8,128)(2,1)}, u32[]{:S(2)}, u32[]{:S(2)}) async-start(bf16[16,512,64]{1,2,0:T(8,128)(2,1)} %fusion.14), calls=%async_computation.1 | async-start | bytes 2097152 | tf_op jit(solution)/shard_map/all_to_all | solution.py:35
  96.2 5.5 copy-start.5
  96.2 5.5 copy-start.6
  96.2 108.5 %all-to-all-start.2 = ((bf16[8,64,1,64,128]{4,3,1,2,0:T(8,128)(2,1)}), bf16[8,64,1,64,128]{4,3,1,2,0:T(8,128)(2,1)}, u32[]{:S(2)}, u32[]{:S(2)}) async-start(bf16[8,64,1,64,128]{4,3,1,2,0:T(8,128)(2,1)} %stack.2), calls=%async_computation.2 | async-start | bytes 16777216 | tf_op jit(solution)/shard_map/all_to_all | solution.py:19
  204.7 14.5 %copy-start.2 = (bf16[64,1,64,128]{3,2,1,0:T(8,128)(2,1)}, bf16[64,1,64,128]{3,2,1,0:T(8,128)(2,1)S(1)}, u32[]{:S(2)}) copy-start(bf16[64,1,64,128]{3,2,1,0:T(8,128)(2,1)S(1)} %get-tuple-element.213) | copy-start | bytes 3145732 | tf_op jit(solution)/shard_map/while
  223.2 3.2 copy-start.4
  228.8 14.5 %copy-start.2 = (bf16[64,1,64,128]{3,2,1,0:T(8,128)(2,1)}, bf16[64,1,64,128]{3,2,1,0:T(8,128)(2,1)S(1)}, u32[]{:S(2)}) copy-start(bf16[64,1,64,128]{3,2,1,0:T(8,128)(2,1)S(1)} %get-tuple-element.213) | copy-start | bytes 3145732 | tf_op jit(solution)/shard_map/while
  252.9 14.5 %copy-start.2 = (bf16[64,1,64,128]{3,2,1,0:T(8,128)(2,1)}, bf16[64,1,64,128]{3,2,1,0:T(8,128)(2,1)S(1)}, u32[]{:S(2)}) copy-start(bf16[64,1,64,128]{3,2,1,0:T(8,128)(2,1)S(1)} %get-tuple-element.213) | copy-start | bytes 3145732 | tf_op jit(solution)/shard_map/while
  277.0 14.5 %copy-start.2 = (bf16[64,1,64,128]{3,2,1,0:T(8,128)(2,1)}, bf16[64,1,64,128]{3,2,1,0:T(8,128)(2,1)S(1)}, u32[]{:S(2)}) copy-start(bf16[64,1,64,128]{3,2,1,0:T(8,128)(2,1)S(1)} %get-tuple-element.213) | copy-start | bytes 3145732 | tf_op jit(solution)/shard_map/while
  301.1 14.4 %copy-start.2 = (bf16[64,1,64,128]{3,2,1,0:T(8,128)(2,1)}, bf16[64,1,64,128]{3,2,1,0:T(8,128)(2,1)S(1)}, u32[]{:S(2)}) copy-start(bf16[64,1,64,128]{3,2,1,0:T(8,128)(2,1)S(1)} %get-tuple-element.213) | copy-start | bytes 3145732 | tf_op jit(solution)/shard_map/while
  325.2 14.5 %copy-start.2 = (bf16[64,1,64,128]{3,2,1,0:T(8,128)(2,1)}, bf16[64,1,64,128]{3,2,1,0:T(8,128)(2,1)S(1)}, u32[]{:S(2)}) copy-start(bf16[64,1,64,128]{3,2,1,0:T(8,128)(2,1)S(1)} %get-tuple-element.213) | copy-start | bytes 3145732 | tf_op jit(solution)/shard_map/while
  349.3 14.5 %copy-start.2 = (bf16[64,1,64,128]{3,2,1,0:T(8,128)(2,1)}, bf16[64,1,64,128]{3,2,1,0:T(8,128)(2,1)S(1)}, u32[]{:S(2)}) copy-start(bf16[64,1,64,128]{3,2,1,0:T(8,128)(2,1)S(1)} %get-tuple-element.213) | copy-start | bytes 3145732 | tf_op jit(solution)/shard_map/while
  373.5 14.5 %copy-start.2 = (bf16[64,1,64,128]{3,2,1,0:T(8,128)(2,1)}, bf16[64,1,64,128]{3,2,1,0:T(8,128)(2,1)S(1)}, u32[]{:S(2)}) copy-start(bf16[64,1,64,128]{3,2,1,0:T(8,128)(2,1)S(1)} %get-tuple-element.213) | copy-start | bytes 3145732 | tf_op jit(solution)/shard_map/while
  391.9 3.2 copy-start.4
  397.6 14.5 %copy-start.2 = (bf16[64,1,64,128]{3,2,1,0:T(8,128)(2,1)}, bf16[64,1,64,128]{3,2,1,0:T(8,128)(2,1)S(1)}, u32[]{:S(2)}) copy-start(bf16[64,1,64,128]{3,2,1,0:T(8,128)(2,1)S(1)} %get-tuple-element.213) | copy-start | bytes 3145732 | tf_op jit(solution)/shard_map/while
  421.7 14.5 %copy-start.2 = (bf16[64,1,64,128]{3,2,1,0:T(8,128)(2,1)}, bf16[64,1,64,128]{3,2,1,0:T(8,128)(2,1)S(1)}, u32[]{:S(2)}) copy-start(bf16[64,1,64,128]{3,2,1,0:T(8,128)(2,1)S(1)} %get-tuple-element.213) | copy-start | bytes 3145732 | tf_op jit(solution)/shard_map/while
  445.8 14.5 %copy-start.2 = (bf16[64,1,64,128]{3,2,1,0:T(8,128)(2,1)}, bf16[64,1,64,128]{3,2,1,0:T(8,128)(2,1)S(1)}, u32[]{:S(2)}) copy-start(bf16[64,1,64,128]{3,2,1,0:T(8,128)(2,1)S(1)} %get-tuple-element.213) | copy-start | bytes 3145732 | tf_op jit(solution)/shard_map/while
  470.0 14.5 %copy-start.2 = (bf16[64,1,64,128]{3,2,1,0:T(8,128)(2,1)}, bf16[64,1,64,128]{3,2,1,0:T(8,128)(2,1)S(1)}, u32[]{:S(2)}) copy-start(bf16[64,1,64,128]{3,2,1,0:T(8,128)(2,1)S(1)} %get-tuple-element.213) | copy-start | bytes 3145732 | tf_op jit(solution)/shard_map/while
  494.1 14.4 %copy-start.2 = (bf16[64,1,64,128]{3,2,1,0:T(8,128)(2,1)}, bf16[64,1,64,128]{3,2,1,0:T(8,128)(2,1)S(1)}, u32[]{:S(2)}) copy-start(bf16[64,1,64,128]{3,2,1,0:T(8,128)(2,1)S(1)} %get-tuple-element.213) | copy-start | bytes 3145732 | tf_op jit(solution)/shard_map/while
  518.2 14.5 %copy-start.2 = (bf16[64,1,64,128]{3,2,1,0:T(8,128)(2,1)}, bf16[64,1,64,128]{3,2,1,0:T(8,128)(2,1)S(1)}, u32[]{:S(2)}) copy-start(bf16[64,1,64,128]{3,2,1,0:T(8,128)(2,1)S(1)} %get-tuple-element.213) | copy-start | bytes 3145732 | tf_op jit(solution)/shard_map/while
  542.2 14.4 %copy-start.2 = (bf16[64,1,64,128]{3,2,1,0:T(8,128)(2,1)}, bf16[64,1,64,128]{3,2,1,0:T(8,128)(2,1)S(1)}, u32[]{:S(2)}) copy-start(bf16[64,1,64,128]{3,2,1,0:T(8,128)(2,1)S(1)} %get-tuple-element.213) | copy-start | bytes 3145732 | tf_op jit(solution)/shard_map/while
  566.3 14.5 %copy-start.2 = (bf16[64,1,64,128]{3,2,1,0:T(8,128)(2,1)}, bf16[64,1,64,128]{3,2,1,0:T(8,128)(2,1)S(1)}, u32[]{:S(2)}) copy-start(bf16[64,1,64,128]{3,2,1,0:T(8,128)(2,1)S(1)} %get-tuple-element.213) | copy-start | bytes 3145732 | tf_op jit(solution)/shard_map/while
  (47 other events, 99.8 us)
Sparse Core Ops, SparseCore 0:
  67.1 65.7 all-gather.2
